TPU v7x, 32 devices: a whole 2x2x4 slice. The times are simulated.
32 devices in a mesh: dp: 4 (over z), expert: 8 (over y, x, core).
Axes of the slice: x: 2, y: 2, z: 4, core: 2. Of those that a mesh axis runs over, the one named last changes fastest.
Arguments:
- tokens: bfloat16 [8, 512, 1024], P('expert', 'dp'), may hold values from -6 to 6
- qkv_weight: bfloat16 [1024, 3072], P(('dp', 'expert')), may hold values from -0.1875 to 0.1875
- proj_weight: bfloat16 [1024, 1024], P(('dp', 'expert')), may hold values from -0.75 to 0.75
- router_weight: bfloat16 [1024, 8], P(('dp', 'expert')), may hold values from -0.09375 to 0.09375
- norm_gains: bfloat16 [2, 1024], P(None, ('dp', 'expert')), may hold values from 0.5 to 1.5
- biases: bfloat16 [5, 1024], P(None, ('dp', 'expert')), may hold values from -1.1953125 to 1.1953125
- up_weight: bfloat16 [8, 1024, 4096], P('expert', None, 'dp'), may hold values from -0.1875 to 0.1875
- up_bias: bfloat16 [8, 4096], P('expert', 'dp'), may hold values from -1.1953125 to 1.1953125
- down_weight: bfloat16 [8, 4096, 1024], P('expert', 'dp'), may hold values from -0.75 to 0.75
- down_bias: bfloat16 [8, 1024], P('expert', 'dp'), may hold values from -6 to 6
- routes: int32 [8, 512, 1], P('expert', 'dp'), may hold values from 0 to 7
- slot_order: int32 [8, 4, 128], P('expert', 'dp'), may hold values from 0 to 127, each once within a row
- segments: int32 [8, 512], P('expert'), may hold values from 0 to 6, never falling along the last dimension, each value on 1 to 256 neighbouring positions
- parents: int32 [8, 7], P('expert'), may hold values from 0 to 5, as said below
- cotangent: bfloat16 [8, 512, 1024], P('expert', 'dp'), may hold values from -6 to 6
Outputs:
- outputs: bfloat16 [8, 512, 1024], P('expert', 'dp')
- grad_tokens: float32 [8, 512, 1024], P('expert', 'dp')
- grad_qkv: float32 [1024, 3072], P(('dp', 'expert'))
- grad_proj: float32 [1024, 1024], P(('dp', 'expert'))
- grad_router: float32 [1024, 8], P(('dp', 'expert'))
- grad_gains: float32 [2, 1024], P(None, ('dp', 'expert'))
- grad_biases: float32 [5, 1024], P(None, ('dp', 'expert'))
- grad_up: float32 [8, 1024, 4096], P('expert', None, 'dp')
- grad_up_bias: float32 [8, 4096], P('expert', 'dp')
- grad_down: float32 [8, 4096, 1024], P('expert', 'dp')
- grad_down_bias: float32 [8, 1024], P('expert', 'dp')
Inputs may be any that keep to these rules, and one draw needn't show every extreme that they name: Along each tree the segment number never falls, every one of the 7 segments has a token, and the longest has 256. parents[t, 0] = 0, parents[t, s] < s for every other s, and the last segment's parent is segment 7 - 2. `routes`: every expert is the route of some token. `slot_order`: each device's 128 tokens hold every priority once.
All inputs are finite; a program needn't handle non-finite values.
Results may differ from a plain program's by a relative error of at most 0.014.
Values may be sent and summed in bfloat16 or wider, within the bound.
No kernel may reach another device: no remote copies, remote signals or barrier semaphores. Data moves between devices by JAX's collectives and lax.ppermute only.
A program may use at most 192 MiB of HBM per device.

v0:
```python
from functools import partial
import math
import jax
import jax.numpy as jnp
from jax import lax
from jax.sharding import PartitionSpec as P

H = 16
NSEG = 7
EPS = 1e-05
NEG = -1e30
HIGH = lax.Precision.HIGHEST


def layer_norm(values, gain, shift):
    mean = jnp.mean(values, axis=-1, keepdims=True)
    centred = values - mean
    spread = jnp.mean(centred * centred, axis=-1, keepdims=True)
    return centred * lax.rsqrt(spread + EPS) * gain + shift


def ancestry(parents, number):
    labels = jnp.arange(number, dtype=jnp.int32)
    direct = (labels[None, :] == parents[:, None]).astype(jnp.float32)
    reach = jnp.minimum(direct + jnp.eye(number, dtype=jnp.float32), 1.0)
    for step in range(3):
        reach = jnp.minimum(jnp.dot(reach, reach, precision=HIGH), 1.0)
    return reach


def slot_table(route_ids, order, experts, capacity):
    labels = jnp.arange(experts, dtype=jnp.int32)
    expert_hot = route_ids[:, None] == labels[None, :]
    same = route_ids[:, None] == route_ids[None, :]
    before = order[None, :] < order[:, None]
    rank = jnp.sum((same & before).astype(jnp.int32), axis=1)
    slot_hot = rank[:, None] == jnp.arange(capacity, dtype=jnp.int32)[None, :]
    table = expert_hot[:, :, None] & slot_hot[:, None, :]
    return (expert_hot.astype(jnp.float32), table)


def expert_gate(logits, expert_hot):
    return jnp.sum(jax.nn.softmax(logits, axis=-1) * expert_hot, axis=-1)


def tanh_gelu(values):
    return jax.nn.gelu(values, approximate=True)


def shards(
    tokens,
    qkv_weight,
    proj_weight,
    router_weight,
    norm_gains,
    biases,
    up_weight,
    up_bias,
    down_weight,
    down_bias,
    routes,
    slot_order,
    segments,
    parents,
    cotangent,
):
    qkv_full, proj_full, router_full, gain_full, bias_full = (
        lax.all_gather(qkv_weight, ("dp", "expert"), axis=0, tiled=True),
        lax.all_gather(proj_weight, ("dp", "expert"), axis=0, tiled=True),
        lax.all_gather(router_weight, ("dp", "expert"), axis=0, tiled=True),
        lax.all_gather(norm_gains, ("dp", "expert"), axis=1, tiled=True),
        lax.all_gather(biases, ("dp", "expert"), axis=1, tiled=True),
    )
    up_full, up_shift, down_full, down_shift = (
        lax.all_gather(up_weight, "dp", axis=2, tiled=True),
        lax.all_gather(up_bias, "dp", axis=1, tiled=True),
        lax.all_gather(down_weight, "dp", axis=1, tiled=True),
        lax.all_gather(down_bias, "dp", axis=1, tiled=True),
    )
    rows = tokens.shape[1]
    width = tokens.shape[2]
    head_dim = width // H
    scale = head_dim ** (-0.5)
    experts = router_full.shape[1]
    capacity = (9 * rows + 8 * experts - 1) // (8 * experts)
    gain32 = gain_full.astype(jnp.float32)
    bias32 = bias_full.astype(jnp.float32)
    inputs = tokens[0].astype(jnp.float32)
    normed, norm1_back = jax.vjp(layer_norm, inputs, gain32[0], bias32[0])
    normed_low = normed.astype(jnp.bfloat16)
    shift = jnp.concatenate([bias32[1], jnp.zeros((width,), jnp.float32), bias32[2]])
    packed = (jnp.dot(normed_low, qkv_full, preferred_element_type=jnp.float32) + shift).astype(
        jnp.bfloat16
    )
    key_value = lax.all_gather(packed[:, width:], "dp", axis=0, tiled=True)
    length = key_value.shape[0]
    start = lax.axis_index("dp") * rows
    query_pos = start + jnp.arange(rows, dtype=jnp.int32)
    reach = ancestry(parents[0], NSEG)
    labels = jnp.arange(NSEG, dtype=jnp.int32)
    key_hot = (segments[0][:, None] == labels[None, :]).astype(jnp.float32)
    query_reach = jnp.dot(lax.dynamic_slice_in_dim(key_hot, start, rows, 0), reach, precision=HIGH)
    block = math.gcd(length, 512)
    number = length // block
    hot_blocks = key_hot.reshape(number, block, NSEG)
    pos_blocks = jnp.arange(length, dtype=jnp.int32).reshape(number, block)
    query_heads = packed[:, :width].reshape(rows, H, head_dim)

    def block_scores(key_blk, hot_blk, pos_blk):
        allowed = (jnp.dot(query_reach, hot_blk.T, precision=HIGH) > 0.5) & (
            pos_blk[None, :] <= query_pos[:, None]
        )
        raw = (
            jnp.einsum("qhd,khd->hqk", query_heads, key_blk, preferred_element_type=jnp.float32)
            * scale
        )
        return jnp.where(allowed[None], raw, NEG)

    def split_blocks(pairs):
        keys = pairs[:, :width].reshape(number, block, H, head_dim)
        values = pairs[:, width:].reshape(number, block, H, head_dim)
        return (keys, values)

    key_blocks, value_blocks = split_blocks(key_value)

    def total_step(carry, item):
        top, total = carry
        scores = block_scores(item[0], item[1], item[2])
        new_top = jnp.maximum(top, jnp.max(scores, axis=-1))
        total = total * jnp.exp(top - new_top) + jnp.sum(
            jnp.exp(scores - new_top[:, :, None]), axis=-1
        )
        return ((new_top, total), None)

    first_carry = (jnp.full((H, rows), NEG, jnp.float32), jnp.zeros((H, rows), jnp.float32))
    (top, total), unused = lax.scan(total_step, first_carry, (key_blocks, hot_blocks, pos_blocks))
    log_total = top + jnp.log(total)

    def value_step(accum, item):
        scores = block_scores(item[0], item[1], item[2])
        probs = jnp.exp(scores - log_total[:, :, None]).astype(jnp.bfloat16)
        return (
            accum + jnp.einsum("hqk,khd->qhd", probs, item[3], preferred_element_type=jnp.float32),
            None,
        )

    attended32, unused = lax.scan(
        value_step,
        jnp.zeros((rows, H, head_dim), jnp.float32),
        (key_blocks, hot_blocks, pos_blocks, value_blocks),
    )
    attended_low = attended32.reshape(rows, width).astype(jnp.bfloat16)
    mixed = (
        inputs + jnp.dot(attended_low, proj_full, preferred_element_type=jnp.float32) + bias32[3]
    )
    normed2, norm2_back = jax.vjp(layer_norm, mixed, gain32[1], bias32[4])
    normed2_low = normed2.astype(jnp.bfloat16)
    logits = jnp.dot(normed2_low, router_full, preferred_element_type=jnp.float32)
    expert_hot, table = slot_table(routes[0, :, 0], slot_order[0, 0], experts, capacity)
    gate, gate_back = jax.vjp(partial(expert_gate, expert_hot=expert_hot), logits)
    table_low = table.astype(jnp.bfloat16)
    sent = jnp.einsum(
        "tec,td->ecd", table_low, normed2_low, preferred_element_type=jnp.float32
    ).astype(jnp.bfloat16)
    arrived = lax.all_to_all(sent, "expert", split_axis=0, concat_axis=0, tiled=True)
    slots = arrived.reshape(-1, width)
    pre = jnp.dot(slots, up_full[0], preferred_element_type=jnp.float32) + up_shift[0].astype(
        jnp.float32
    )
    act, act_back = jax.vjp(tanh_gelu, pre)
    act_low = act.astype(jnp.bfloat16)
    result = (
        jnp.dot(act_low, down_full[0], preferred_element_type=jnp.float32)
        + down_shift[0].astype(jnp.float32)
    ).astype(jnp.bfloat16)
    returned = lax.all_to_all(
        result.reshape(arrived.shape), "expert", split_axis=0, concat_axis=0, tiled=True
    )
    combined = jnp.einsum("tec,ecd->td", table_low, returned, preferred_element_type=jnp.float32)
    outputs = (mixed + gate[:, None] * combined).astype(jnp.bfloat16)
    qkv_full, proj_full, router_full = (
        lax.all_gather(qkv_weight, ("dp", "expert"), axis=0, tiled=True),
        lax.all_gather(proj_weight, ("dp", "expert"), axis=0, tiled=True),
        lax.all_gather(router_weight, ("dp", "expert"), axis=0, tiled=True),
    )
    up_full, down_full = (
        lax.all_gather(up_weight, "dp", axis=2, tiled=True),
        lax.all_gather(down_weight, "dp", axis=1, tiled=True),
    )
    key_value = lax.all_gather(packed[:, width:], "dp", axis=0, tiled=True)
    key_blocks, value_blocks = split_blocks(key_value)
    upstream = cotangent[0].astype(jnp.float32)
    d_gate = jnp.sum(upstream * combined, axis=-1)
    table32 = table.astype(jnp.float32)
    d_result = jnp.einsum("tec,td->ecd", table32, gate[:, None] * upstream, precision=HIGH).astype(
        jnp.bfloat16
    )
    d_arrived = lax.all_to_all(d_result, "expert", split_axis=0, concat_axis=0, tiled=True)
    d_rows = d_arrived.reshape(-1, width)
    grad_down_bias = jnp.sum(d_rows.astype(jnp.float32), axis=0)
    grad_down = jnp.einsum("rf,rd->fd", act_low, d_rows, preferred_element_type=jnp.float32)
    d_act = jnp.einsum("rd,fd->rf", d_rows, down_full[0], preferred_element_type=jnp.float32)
    d_pre = act_back(d_act)[0]
    grad_up_bias = jnp.sum(d_pre, axis=0)
    d_pre_low = d_pre.astype(jnp.bfloat16)
    grad_up = jnp.einsum("rd,rf->df", slots, d_pre_low, preferred_element_type=jnp.float32)
    d_slots = jnp.einsum(
        "rf,df->rd", d_pre_low, up_full[0], preferred_element_type=jnp.float32
    ).astype(jnp.bfloat16)
    d_sent = lax.all_to_all(
        d_slots.reshape(arrived.shape), "expert", split_axis=0, concat_axis=0, tiled=True
    )
    d_logits = gate_back(d_gate)[0]
    grad_router = jnp.einsum("td,te->de", normed2_low.astype(jnp.float32), d_logits, precision=HIGH)
    d_normed2 = jnp.einsum("tec,ecd->td", table_low, d_sent, preferred_element_type=jnp.float32)
    d_normed2 = d_normed2 + jnp.einsum(
        "te,de->td", d_logits, router_full.astype(jnp.float32), precision=HIGH
    )
    d_mixed_norm, grad_gain_second, grad_shift_norm2 = norm2_back(d_normed2)
    d_mixed = upstream + d_mixed_norm
    grad_shift_proj = jnp.sum(d_mixed, axis=0)
    d_mixed_low = d_mixed.astype(jnp.bfloat16)
    grad_proj = jnp.einsum(
        "tc,td->cd", attended_low, d_mixed_low, preferred_element_type=jnp.float32
    )
    d_attended = jnp.einsum(
        "td,cd->tc", d_mixed_low, proj_full, preferred_element_type=jnp.float32
    ).astype(jnp.bfloat16)
    d_heads = d_attended.reshape(rows, H, head_dim)
    delta = jnp.einsum("qhd,qhd->hq", d_heads.astype(jnp.float32), attended32, precision=HIGH)

    def grad_step(d_query, item):
        scores = block_scores(item[0], item[1], item[2])
        probs = jnp.exp(scores - log_total[:, :, None])
        probs_low = probs.astype(jnp.bfloat16)
        d_value = jnp.einsum("hqk,qhd->khd", probs_low, d_heads, preferred_element_type=jnp.float32)
        d_probs = jnp.einsum("qhd,khd->hqk", d_heads, item[3], preferred_element_type=jnp.float32)
        d_scores = (probs * (d_probs - delta[:, :, None])).astype(jnp.bfloat16)
        d_query = d_query + jnp.einsum(
            "hqk,khd->qhd", d_scores, item[0], preferred_element_type=jnp.float32
        )
        d_key = (
            jnp.einsum("hqk,qhd->khd", d_scores, query_heads, preferred_element_type=jnp.float32)
            * scale
        )
        joined = jnp.concatenate(
            [d_key.reshape(block, width), d_value.reshape(block, width)], axis=1
        )
        return (d_query, joined)

    d_query, joined = lax.scan(
        grad_step,
        jnp.zeros((rows, H, head_dim), jnp.float32),
        (key_blocks, hot_blocks, pos_blocks, value_blocks),
    )
    joined_rows = joined.reshape(length, 2 * width)
    d_key_value = lax.psum_scatter(
        joined_rows.astype(jnp.bfloat16), "dp", scatter_dimension=0, tiled=True
    ).astype(jnp.float32)
    d_packed = jnp.concatenate(
        [(d_query * scale).reshape(rows, width), d_key_value], axis=1
    ).astype(jnp.bfloat16)
    packed_sums = jnp.sum(d_packed.astype(jnp.float32), axis=0)
    grad_qkv = jnp.einsum("tc,te->ce", normed_low, d_packed, preferred_element_type=jnp.float32)
    d_normed = jnp.einsum("te,ce->tc", d_packed, qkv_full, preferred_element_type=jnp.float32)
    d_inputs, grad_gain_first, grad_shift_norm1 = norm1_back(d_normed)
    grad_tokens = d_mixed + d_inputs
    grad_gains = jnp.stack([grad_gain_first, grad_gain_second])
    grad_biases = jnp.stack(
        [
            grad_shift_norm1,
            packed_sums[:width],
            packed_sums[2 * width :],
            grad_shift_proj,
            grad_shift_norm2,
        ]
    )
    owned_qkv, owned_proj, owned_router, owned_gains, owned_biases = (
        lax.psum_scatter(grad_qkv, ("dp", "expert"), scatter_dimension=0, tiled=True),
        lax.psum_scatter(grad_proj, ("dp", "expert"), scatter_dimension=0, tiled=True),
        lax.psum_scatter(grad_router, ("dp", "expert"), scatter_dimension=0, tiled=True),
        lax.psum_scatter(grad_gains, ("dp", "expert"), scatter_dimension=1, tiled=True),
        lax.psum_scatter(grad_biases, ("dp", "expert"), scatter_dimension=1, tiled=True),
    )
    owned_up, owned_up_bias, owned_down, owned_down_bias = (
        lax.psum_scatter(
            grad_up[None].astype(jnp.bfloat16), "dp", scatter_dimension=2, tiled=True
        ).astype(jnp.float32),
        lax.psum_scatter(
            grad_up_bias[None].astype(jnp.bfloat16), "dp", scatter_dimension=1, tiled=True
        ).astype(jnp.float32),
        lax.psum_scatter(
            grad_down[None].astype(jnp.bfloat16), "dp", scatter_dimension=1, tiled=True
        ).astype(jnp.float32),
        lax.psum_scatter(
            grad_down_bias[None].astype(jnp.bfloat16), "dp", scatter_dimension=1, tiled=True
        ).astype(jnp.float32),
    )
    return (
        outputs[None],
        grad_tokens[None],
        owned_qkv,
        owned_proj,
        owned_router,
        owned_gains,
        owned_biases,
        owned_up,
        owned_up_bias,
        owned_down,
        owned_down_bias,
    )


def solution(mesh):
    placed = (
        P("expert", "dp", None),
        P(("dp", "expert"), None),
        P(("dp", "expert"), None),
        P(("dp", "expert"), None),
        P(None, ("dp", "expert")),
        P(None, ("dp", "expert")),
        P("expert", None, "dp"),
        P("expert", "dp"),
        P("expert", "dp", None),
        P("expert", "dp"),
        P("expert", "dp", None),
        P("expert", "dp", None),
        P("expert", None),
        P("expert", None),
        P("expert", "dp", None),
    )
    return jax.shard_map(
        shards,
        mesh=mesh,
        in_specs=placed,
        out_specs=(
            P("expert", "dp", None),
            P("expert", "dp", None),
            P(("dp", "expert"), None),
            P(("dp", "expert"), None),
            P(("dp", "expert"), None),
            P(None, ("dp", "expert")),
            P(None, ("dp", "expert")),
            P("expert", None, "dp"),
            P("expert", "dp"),
            P("expert", "dp", None),
            P("expert", "dp"),
        ),
        check_vma=False,
    )
```

profile of v0, /device:TPU:0, one launch (start us, length us, event | category | flops | bytes accessed | tf_op | source)
XLA Modules:
  0.0 1658.2 jit_solution(5418637222346388384)
XLA Ops:
  8.0 43.2 %all-gather = bf16[32,32,2]{1,2,0:T(2,128)(2,1)S(1)} all-gather(bf16[1,32,2]{1,2,0:T(2,128)(2,1)} %bitcast.257), channel_id=1, replica_groups=mesh['dp'=4,'expert'=8] {'dp','expert'}, dimensions={0}, use_global_device_ids=true | all-gather | bytes 4224 | tf_op jit(solution)/shard_map/all_gather | solution.py:71
  51.3 37.4 %all-gather.1 = bf16[32,32,5]{1,2,0:T(8,128)(2,1)S(1)} all-gather(bf16[1,32,5]{1,2,0:T(8,128)(2,1)} %bitcast.252), channel_id=1, replica_groups=mesh['dp'=4,'expert'=8] {'dp','expert'}, dimensions={0}, use_global_device_ids=true | all-gather | bytes 10560 | tf_op jit(solution)/shard_map/all_gather | solution.py:72
  99.6 40.3 %all-gather.11.cloned.1.call-done = bf16[512,2048]{1,0:T(8,128)(2,1)} async-done(((bf16[128,2048]{1,0:T(8,128)(2,1)}), bf16[512,2048]{1,0:T(8,128)(2,1)}) %all-gather.11.cloned.1.call-update) | async-done | bytes 2097168 | tf_op jit(solution)/shard_map/all_gather | solution.py:95
  147.7 50.2 %all-gather.13.cloned.1.call-done = bf16[1024,1024]{1,0:T(8,128)(2,1)} async-done(((bf16[32,1024]{1,0:T(8,128)(2,1)}), bf16[1024,1024]{1,0:T(8,128)(2,1)}) %all-gather.13.cloned.1.call-update) | async-done | bytes 2097168 | tf_op jit(solution)/shard_map/all_gather | solution.py:69
  205.0 9.8 all_gather.45
  214.8 15.4 all_gather.43
  230.2 41.5 %all-gather.2 = bf16[32,32,8]{1,2,0:T(8,128)(2,1)S(1)} all-gather(bf16[1,32,8]{1,2,0:T(8,128)(2,1)S(1)} %bitcast.255), channel_id=1, replica_groups=mesh['dp'=4,'expert'=8] {'dp','expert'}, dimensions={0}, use_global_device_ids=true | all-gather | bytes 16896 | tf_op jit(solution)/shard_map/all_gather | solution.py:70
  272.2 76.2 %all-gather.15.cloned.1.call-done = bf16[1,1024,4096]{2,1,0:T(8,128)(2,1)} async-done(((bf16[1,1024,1024]{2,1,0:T(8,128)(2,1)}), bf16[1,1024,4096]{2,1,0:T(8,128)(2,1)}) %all-gather.15.cloned.1.call-update) | async-done | bytes 8388624 | tf_op jit(solution)/shard_map/all_gather | solution.py:75
  354.6 143.1 %all-gather.17.cloned.1.call-done = bf16[1,4096,1024]{2,1,0:T(8,128)(2,1)} async-done(((bf16[1,1024,1024]{2,1,0:T(8,128)(2,1)}), bf16[1,4096,1024]{2,1,0:T(8,128)(2,1)}) %all-gather.17.cloned.1.call-update) | async-done | bytes 8388624 | tf_op jit(solution)/shard_map/all_gather | solution.py:77
  508.1 8.3 all-to-all-done.1
  517.4 10.7 all_to_all.20
  528.2 8.0 fusion.114
  548.2 8.0 all-to-all-done.3
  577.1 32.7 %reduce-scatter.31.cloned.1.call-done = bf16[128,2048]{1,0:T(8,128)(2,1)} async-done(((bf16[512,2048]{1,0:T(8,128)(2,1)}), bf16[128,2048]{1,0:T(8,128)(2,1)}) %reduce-scatter.31.cloned.1.call-update) | async-done | bytes 524304
  621.4 7.3 convert_bitcast_fusion
  647.0 98.7 %reduce-scatter.33.cloned.1.call-done = f32[32,8]{1,0:T(8,128)} async-done(((f32[1024,8]{1,0:T(8,128)}), f32[32,8]{1,0:T(8,128)}) %reduce-scatter.33.cloned.1.call-update) | async-done | bytes 1040
  747.0 16.5 reduce-scatter.41.cloned.1.call-done
  765.0 26.3 %reduce-scatter.39.cloned.1.call-done = bf16[1024,1]{1,0:T(8,128)(2,1)} async-done(((bf16[4096,1]{1,0:T(8,128)(2,1)}), bf16[1024,1]{1,0:T(8,128)(2,1)}) %reduce-scatter.39.cloned.1.call-update) | async-done | bytes 2064
  793.0 133.7 %reduce-scatter.35.cloned.1.call-done = f32[32,2]{1,0:T(8,128)} async-done(((f32[1024,2]{1,0:T(8,128)}), f32[32,2]{1,0:T(8,128)}) %reduce-scatter.35.cloned.1.call-update) | async-done | bytes 272
  928.0 130.7 %reduce-scatter.37.cloned.1.call-done = f32[32,5]{1,0:T(8,128)} async-done(((f32[1024,5]{1,0:T(8,128)}), f32[32,5]{1,0:T(8,128)}) %reduce-scatter.37.cloned.1.call-update) | async-done | bytes 656
  1060.0 141.2 %reduce-scatter.29.cloned.1.call-done = bf16[1,1024,1024]{2,1,0:T(8,128)(2,1)} async-done(((bf16[1,4096,1024]{2,1,0:T(8,128)(2,1)}), bf16[1,1024,1024]{2,1,0:T(8,128)(2,1)}) %reduce-scatter.29.cloned.1.call-update) | async-done | bytes 2097168 | tf_op jit(solution)/shard_map/reduce_scatter | solution.py:292
  1205.3 143.5 %reduce-scatter.27.cloned.1.call-done = bf16[1,1024,1024]{2,1,0:T(8,128)(2,1)} async-done(((bf16[1,1024,4096]{2,1,0:T(8,128)(2,1)}), bf16[1,1024,1024]{2,1,0:T(8,128)(2,1)}) %reduce-scatter.27.cloned.1.call-update) | async-done | bytes 2097168 | tf_op jit(solution)/shard_map/reduce_scatter | solution.py:286
  1352.9 140.4 %reduce-scatter.25.cloned.1.call-done = f32[32,1024]{1,0:T(8,128)} async-done(((f32[1024,1024]{1,0:T(8,128)}), f32[32,1024]{1,0:T(8,128)}) %reduce-scatter.25.cloned.1.call-update) | async-done | bytes 131088 | tf_op jit(solution)/shard_map/reduce_scatter | solution.py:280
  1493.3 158.1 %reduce-scatter.23.cloned.1.call-done = f32[32,3072]{1,0:T(8,128)} async-done(((f32[1024,3072]{1,0:T(8,128)}), f32[32,3072]{1,0:T(8,128)}) %reduce-scatter.23.cloned.1.call-update) | async-done | bytes 393232 | tf_op jit(solution)/shard_map/reduce_scatter | solution.py:279
  (201 shorter events, 122.1 us)
Async XLA Ops:
  7.2 84.0 %all-gather.9.cloned.1.call-start = ((), (), s32[]{:S(2)}) async-start(), calls=%async_computation.14 | async-start | bytes 6488064 | tf_op jit(solution)/shard_map/all_gather | solution.py:68
  7.9 132.0 %all-gather.11.cloned.1.call-start = ((), (), s32[]{:S(2)}) async-start(), calls=%async_computation.15 | async-start | bytes 2621440 | tf_op jit(solution)/shard_map/all_gather | solution.py:95
  96.0 101.9 %all-gather.13.cloned.1.call-start = ((), (), s32[]{:S(2)}) async-start(), calls=%async_computation.16 | async-start | bytes 2162688 | tf_op jit(solution)/shard_map/all_gather | solution.py:69
  96.7 251.7 %all-gather.15.cloned.1.call-start = ((), (), s32[]{:S(2)}) async-start(), calls=%async_computation.17 | async-start | bytes 10485760 | tf_op jit(solution)/shard_map/all_gather | solution.py:75
  97.3 400.4 %all-gather.17.cloned.1.call-start = ((), (), s32[]{:S(2)}) async-start(), calls=%async_computation.18 | async-start | bytes 10485760 | tf_op jit(solution)/shard_map/all_gather | solution.py:77
  99.6 43.1 %copy-start.17 = (bf16[128,1024]{0,1:T(8,128)(2,1)}, bf16[128,1024]{0,1:T(8,128)(2,1)S(1)}, u32[]{:S(2)}) copy-start(bf16[128,1024]{0,1:T(8,128)(2,1)S(1)} %copy.58) | copy-start | bytes 786436
  145.7 52.2 %copy-start.2 = (bf16[1,128,1024]{2,1,0:T(8,128)(2,1)S(1)}, bf16[1,128,1024]{2,1,0:T(8,128)(2,1)}, u32[]{:S(2)}) copy-start(bf16[1,128,1024]{2,1,0:T(8,128)(2,1)} %param.15) | copy-start | bytes 786436
  147.7 52.6 %copy-start.21 = (bf16[128,16,64]{0,2,1:T(8,128)(2,1)}, bf16[128,16,64]{0,2,1:T(8,128)(2,1)S(1)}, u32[]{:S(2)}) copy-start(bf16[128,16,64]{0,2,1:T(8,128)(2,1)S(1)} %get-tuple-element.134) | copy-start | bytes 786436
  197.9 32.3 %copy-start.29 = (bf16[32,8]{0,1:T(8,128)(2,1)S(1)}, bf16[32,8]{0,1:T(8,128)(2,1)}, u32[]{:S(2)}) copy-start(bf16[32,8]{0,1:T(8,128)(2,1)} %param.18) | copy-start | bytes 1540
  200.5 154.1 %copy-start.12 = (bf16[128,1024]{1,0:T(8,128)(2,1)}, bf16[128,1024]{1,0:T(8,128)(2,1)S(1)}, u32[]{:S(2)}) copy-start(bf16[128,1024]{1,0:T(8,128)(2,1)S(1)} %add_convert_fusion.1) | copy-start | bytes 786436
  201.5 70.5 %all-to-all-start = ((bf16[8,18,1024]{2,1,0:T(8,128)(2,1)}), bf16[8,18,1024]{2,1,0:T(8,128)(2,1)S(1)}, u32[]{:S(2)}, u32[]{:S(2)}) async-start(bf16[8,18,1024]{2,1,0:T(8,128)(2,1)} %convolution_convert_fusion.2), calls=%async_computation | async-start | bytes 786432 | tf_op jit(solution)/shard_map/all_to_all | solution.py:165
  272.1 82.4 %copy-start.13 = (bf16[144,1024]{1,0:T(8,128)(2,1)}, bf16[144,1024]{1,0:T(8,128)(2,1)S(1)}, u32[]{:S(2)}) copy-start(bf16[144,1024]{1,0:T(8,128)(2,1)S(1)} %reshape.239) | copy-start | bytes 884740
  504.4 12.0 all-to-all-start.1
  544.5 11.7 all-to-all-start.3
  548.0 61.9 %reduce-scatter.31.cloned.1.call-start = ((), (), s32[]{:S(2)}) async-start(), calls=%async_computation.23 | async-start | bytes 2621440
  569.4 176.2 %reduce-scatter.33.cloned.1.call-start = ((), (), s32[]{:S(2)}) async-start(), calls=%async_computation.24 | async-start | bytes 540672
  571.8 191.7 %reduce-scatter.41.cloned.1.call-start = ((), (), s32[]{:S(2)}) async-start(), calls=%async_computation.28 | async-start | bytes 327680
  573.9 217.4 %reduce-scatter.39.cloned.1.call-start = ((), (), s32[]{:S(2)}) async-start(), calls=%async_computation.27 | async-start | bytes 1310720
  575.6 351.1 %reduce-scatter.35.cloned.1.call-start = ((), (), s32[]{:S(2)}) async-start(), calls=%async_computation.25 | async-start | bytes 540672
  619.1 439.5 %reduce-scatter.37.cloned.1.call-start = ((), (), s32[]{:S(2)}) async-start(), calls=%async_computation.26 | async-start | bytes 540672
  621.4 579.9 %reduce-scatter.29.cloned.1.call-start = ((), (), s32[]{:S(2)}) async-start(), calls=%async_computation.22 | async-start | bytes 10485760 | tf_op jit(solution)/shard_map/reduce_scatter | solution.py:292
  628.8 720.1 %reduce-scatter.27.cloned.1.call-start = ((), (), s32[]{:S(2)}) async-start(), calls=%async_computation.21 | async-start | bytes 10485760 | tf_op jit(solution)/shard_map/reduce_scatter | solution.py:286
  635.8 857.5 %reduce-scatter.25.cloned.1.call-start = ((), (), s32[]{:S(2)}) async-start(), calls=%async_computation.20 | async-start | bytes 4325376 | tf_op jit(solution)/shard_map/reduce_scatter | solution.py:280
  639.5 1011.9 %reduce-scatter.23.cloned.1.call-start = ((), (), s32[]{:S(2)}) async-start(), calls=%async_computation.19 | async-start | bytes 12976128 | tf_op jit(solution)/shard_map/reduce_scatter | solution.py:279
  (27 other events, 116.2 us)
Sparse Core Ops, SparseCore 0:
  10.9 71.9 all-gather.8
  96.1 43.7 all-gather.10
  142.8 55.0 all-gather.12
  199.3 149.0 all-gather.14
  349.8 147.8 all-gather.16
  569.5 40.3 reduce-scatter.30
  612.2 133.3 reduce-scatter.32
  747.9 15.5 reduce-scatter.40
  765.9 25.3 reduce-scatter.38
  793.9 132.6 reduce-scatter.34
  929.0 129.6 reduce-scatter.36
  1060.9 140.3 reduce-scatter.28
  1203.6 145.1 reduce-scatter.26
  1351.6 141.6 reduce-scatter.24
  1499.7 151.6 reduce-scatter.22
where the time goes:
time: 1670 us; the launch traced here: 1660 us
  waiting for transfers between devices  1350 us (81%)
  blocking collectives  158 us (9%)
  matrix products  77.5 us (5%)
  local copies, waits for them, and re-layouts  27.1 us (2%)
  other arithmetic  18.6 us (1%)
    unnamed x21, waiting for transfers between devices  441 us
    reduce_scatter x1, waiting for transfers between devices, shards(): lax.psum_scatter(grad_qkv, ('dp', 'expert'), scatter_dimension=0, tiled=T...  158 us
    reduce_scatter x1, waiting for transfers between devices, shards(): lax.psum_scatter(grad_up[None].astype(jnp.bfloat16), 'dp', scatter_dimens...  144 us
    all_gather x1, waiting for transfers between devices, shards(): lax.all_gather(down_weight, 'dp', axis=1, tiled=True)  143 us
    reduce_scatter x1, waiting for transfers between devices, shards(): lax.psum_scatter(grad_down[None].astype(jnp.bfloat16), 'dp', scatter_dime...  141 us
    reduce_scatter x1, waiting for transfers between devices, shards(): lax.psum_scatter(grad_proj, ('dp', 'expert'), scatter_dimension=0, tiled=...  140 us
    all_gather x1, waiting for transfers between devices, shards(): lax.all_gather(up_weight, 'dp', axis=2, tiled=True)  76.2 us
    all_gather x1, waiting for transfers between devices, shards(): lax.all_gather(proj_weight, ('dp', 'expert'), axis=0, tiled=True)  50.2 us
  transfers between devices with their start and end apart: 18, of which 16 were waited for; matrix products, arithmetic and copies ran while one was open for 5% of the time, Pallas kernels for 0%

commit v1 on v0

--- a/solution.py
+++ b/solution.py
@@ -10,6 +10,27 @@
 EPS = 1e-05
 NEG = -1e30
 HIGH = lax.Precision.HIGHEST
+
+
+def collect(array, axis, dim):
+    size, index, rows = (lax.axis_size(axis), lax.axis_index(axis), array.shape[dim])
+    right = [(i, (i + 1) % size) for i in range(size)]
+    left = [(i, (i - 1) % size) for i in range(size)]
+    whole = jnp.zeros((*array.shape[:dim], size * rows, *array.shape[dim + 1 :]), array.dtype)
+    whole = lax.dynamic_update_slice_in_dim(whole, array, index * rows, axis=dim)
+    from_left = from_right = array
+    half = size // 2
+    for step in range(1, half + 1):
+        from_left = lax.ppermute(from_left, axis, right)
+        whole = lax.dynamic_update_slice_in_dim(
+            whole, from_left, (index - step) % size * rows, axis=dim
+        )
+        if step < size - half:
+            from_right = lax.ppermute(from_right, axis, left)
+            whole = lax.dynamic_update_slice_in_dim(
+                whole, from_right, (index + step) % size * rows, axis=dim
+            )
+    return whole
 
 
 def layer_norm(values, gain, shift):
@@ -72,7 +93,7 @@
         lax.all_gather(biases, ("dp", "expert"), axis=1, tiled=True),
     )
     up_full, up_shift, down_full, down_shift = (
-        lax.all_gather(up_weight, "dp", axis=2, tiled=True),
+        collect(up_weight, "dp", 2),
         lax.all_gather(up_bias, "dp", axis=1, tiled=True),
         lax.all_gather(down_weight, "dp", axis=1, tiled=True),
         lax.all_gather(down_bias, "dp", axis=1, tiled=True),

time: 1670 us -> 1740 us (1.042)
  blocking collectives: 158 us -> 271 us
  waiting for transfers between devices: 1350 us -> 1280 us
  local copies, waits for them, and re-layouts: 27.1 us -> 45.2 us
    all_gather x1, blocking collectives: 15.4 us -> 133 us  [shards(): lax.all_gather(up_bias, 'dp', axis=1, tiled=True)]
    all_gather x1, waiting for transfers between devices: 143 us -> 62.8 us  [shards(): lax.all_gather(down_weight, 'dp', axis=1, tiled=True)]
    ppermute x0 -> x3, waiting for transfers between devices: none -> 69.5 us  [the longest x2 69.5 us: collect(): from_left = lax.ppermute(from_left, axis, right)]
    all_gather x1, waiting for transfers between devices: 50.2 us -> 0.02 us  [shards(): lax.all_gather(proj_weight, ('dp', 'expert'), axis=0, tiled=True)]
    all_gather x1, waiting for transfers between devices: 40.3 us -> 0.02 us  [shards(): key_value = lax.all_gather(packed[:, width:], 'dp', axis=0, tiled=True)]
    all_gather x1, waiting for transfers between devices: 76.2 us -> 109 us  [shards(): lax.all_gather(up_weight, 'dp', axis=2, tiled=True)]
  transfers between devices with their start and end apart: 18 -> 21, of which waited for: 16 -> 15; matrix products, arithmetic and copies ran while one was open for 5% -> 7% of each run, Pallas kernels for 0% -> 0%
where the time goes in v1:
time: 1740 us; the launch traced here: 1730 us
  waiting for transfers between devices  1280 us (74%)
  blocking collectives  271 us (16%)
  matrix products  81.5 us (5%)
  local copies, waits for them, and re-layouts  45.2 us (3%)
  other arithmetic  19.2 us (1%)
    unnamed x21, waiting for transfers between devices  441 us
    reduce_scatter x1, waiting for transfers between devices, shards(): lax.psum_scatter(grad_qkv, ('dp', 'expert'), scatter_dimension=0, tiled=T...  158 us
    reduce_scatter x1, waiting for transfers between devices, shards(): lax.psum_scatter(grad_up[None].astype(jnp.bfloat16), 'dp', scatter_dimens...  143 us
    reduce_scatter x1, waiting for transfers between devices, shards(): lax.psum_scatter(grad_down[None].astype(jnp.bfloat16), 'dp', scatter_dime...  141 us
    reduce_scatter x1, waiting for transfers between devices, shards(): lax.psum_scatter(grad_proj, ('dp', 'expert'), scatter_dimension=0, tiled=...  140 us
    all_gather x1, blocking collectives, shards(): lax.all_gather(up_bias, 'dp', axis=1, tiled=True)  133 us
    all_gather x1, waiting for transfers between devices, shards(): lax.all_gather(up_weight, 'dp', axis=2, tiled=True)  109 us
    ppermute x2, waiting for transfers between devices, collect(): from_left = lax.ppermute(from_left, axis, right)  69.5 us
  transfers between devices with their start and end apart: 21, of which 15 were waited for; matrix products, arithmetic and copies ran while one was open for 7% of the time, Pallas kernels for 0%

profile of v1, /device:TPU:0, one launch (start us, length us, event | category | flops | bytes accessed | tf_op | source)
XLA Modules:
  0.0 1729.1 jit_solution(5984895198949414510)
XLA Ops:
  8.0 43.9 %all-gather.1 = bf16[32,32,5]{1,2,0:T(8,128)(2,1)S(1)} all-gather(bf16[1,32,5]{1,2,0:T(8,128)(2,1)} %bitcast.257), channel_id=1, replica_groups=mesh['dp'=4,'expert'=8] {'dp','expert'}, dimensions={0}, use_global_device_ids=true | all-gather | bytes 10560 | tf_op jit(solution)/shard_map/all_gather | solution.py:93
  51.9 36.8 %all-gather = bf16[32,32,2]{1,2,0:T(2,128)(2,1)S(1)} all-gather(bf16[1,32,2]{1,2,0:T(2,128)(2,1)} %bitcast.262), channel_id=1, replica_groups=mesh['dp'=4,'expert'=8] {'dp','expert'}, dimensions={0}, use_global_device_ids=true | all-gather | bytes 4224 | tf_op jit(solution)/shard_map/all_gather | solution.py:92
  101.8 133.0 %all_gather.41 = bf16[1,4096]{1,0:T(2,128)(2,1)S(1)} all-gather(bf16[1,1024]{1,0:T(2,128)(2,1)S(1)} %copy-done.31), channel_id=1, replica_groups=mesh['dp'=4,'expert'=8] {'dp'}, dimensions={1}, use_global_device_ids=true | all-gather | bytes 10240 | tf_op jit(solution)/shard_map/all_gather | solution.py:97
  234.9 7.9 all_gather.43
  243.5 38.3 %all-gather.2 = bf16[32,32,8]{1,2,0:T(8,128)(2,1)S(1)} all-gather(bf16[1,32,8]{1,2,0:T(8,128)(2,1)S(1)} %bitcast.258), channel_id=1, replica_groups=mesh['dp'=4,'expert'=8] {'dp','expert'}, dimensions={0}, use_global_device_ids=true | all-gather | bytes 16896 | tf_op jit(solution)/shard_map/all_gather | solution.py:91
  315.2 69.5 %collective-permute-done.2 = bf16[1,1024,1024]{2,1,0:T(8,128)(2,1)} collective-permute-done((bf16[1,1024,1024]{2,1,0:T(8,128)(2,1)}, bf16[1,1024,1024]{2,1,0:T(8,128)(2,1)}, u32[]{:S(2)}, u32[]{:S(2)}) %collective-permute-start.2) | collective-permute-done | bytes 2097184 | tf_op jit(solution)/shard_map/ppermute | solution.py:24
  394.4 62.8 %all-gather.15.cloned.1.call-done = bf16[1,4096,1024]{2,1,0:T(8,128)(2,1)} async-done(((bf16[1,1024,1024]{2,1,0:T(8,128)(2,1)}), bf16[1,4096,1024]{2,1,0:T(8,128)(2,1)}) %all-gather.15.cloned.1.call-update) | async-done | bytes 8388624 | tf_op jit(solution)/shard_map/all_gather | solution.py:98
  467.6 8.3 all-to-all-done.1
  477.7 10.7 all_to_all.20
  490.0 8.0 fusion.109
  498.0 108.6 %all-gather.17.cloned.1.call-done = bf16[1,1024,4096]{2,1,0:T(8,128)(2,1)} async-done(((bf16[1,1024,1024]{2,1,0:T(8,128)(2,1)}), bf16[1,1024,4096]{2,1,0:T(8,128)(2,1)}) %all-gather.17.cloned.1.call-update) | async-done | bytes 8388624 | tf_op jit(solution)/shard_map/all_gather | solution.py:208
  606.6 7.0 fusion.24
  619.4 8.1 all-to-all-done.3
  648.4 32.7 %reduce-scatter.31.cloned.1.call-done = bf16[128,2048]{1,0:T(8,128)(2,1)} async-done(((bf16[512,2048]{1,0:T(8,128)(2,1)}), bf16[128,2048]{1,0:T(8,128)(2,1)}) %reduce-scatter.31.cloned.1.call-update) | async-done | bytes 524304
  692.7 7.3 convert_bitcast_fusion
  718.1 98.7 %reduce-scatter.33.cloned.1.call-done = f32[32,8]{1,0:T(8,128)} async-done(((f32[1024,8]{1,0:T(8,128)}), f32[32,8]{1,0:T(8,128)}) %reduce-scatter.33.cloned.1.call-update) | async-done | bytes 1040
  818.2 16.5 reduce-scatter.41.cloned.1.call-done
  836.2 26.3 %reduce-scatter.39.cloned.1.call-done = bf16[1024,1]{1,0:T(8,128)(2,1)} async-done(((bf16[4096,1]{1,0:T(8,128)(2,1)}), bf16[1024,1]{1,0:T(8,128)(2,1)}) %reduce-scatter.39.cloned.1.call-update) | async-done | bytes 2064
  864.2 133.4 %reduce-scatter.35.cloned.1.call-done = f32[32,2]{1,0:T(8,128)} async-done(((f32[1024,2]{1,0:T(8,128)}), f32[32,2]{1,0:T(8,128)}) %reduce-scatter.35.cloned.1.call-update) | async-done | bytes 272
  999.0 131.0 %reduce-scatter.37.cloned.1.call-done = f32[32,5]{1,0:T(8,128)} async-done(((f32[1024,5]{1,0:T(8,128)}), f32[32,5]{1,0:T(8,128)}) %reduce-scatter.37.cloned.1.call-update) | async-done | bytes 656
  1131.3 141.2 %reduce-scatter.29.cloned.1.call-done = bf16[1,1024,1024]{2,1,0:T(8,128)(2,1)} async-done(((bf16[1,4096,1024]{2,1,0:T(8,128)(2,1)}), bf16[1,1024,1024]{2,1,0:T(8,128)(2,1)}) %reduce-scatter.29.cloned.1.call-update) | async-done | bytes 2097168 | tf_op jit(solution)/shard_map/reduce_scatter | solution.py:313
  1276.6 143.5 %reduce-scatter.27.cloned.1.call-done = bf16[1,1024,1024]{2,1,0:T(8,128)(2,1)} async-done(((bf16[1,1024,4096]{2,1,0:T(8,128)(2,1)}), bf16[1,1024,1024]{2,1,0:T(8,128)(2,1)}) %reduce-scatter.27.cloned.1.call-update) | async-done | bytes 2097168 | tf_op jit(solution)/shard_map/reduce_scatter | solution.py:307
  1424.2 140.4 %reduce-scatter.25.cloned.1.call-done = f32[32,1024]{1,0:T(8,128)} async-done(((f32[1024,1024]{1,0:T(8,128)}), f32[32,1024]{1,0:T(8,128)}) %reduce-scatter.25.cloned.1.call-update) | async-done | bytes 131088 | tf_op jit(solution)/shard_map/reduce_scatter | solution.py:301
  1564.6 157.7 %reduce-scatter.23.cloned.1.call-done = f32[32,3072]{1,0:T(8,128)} async-done(((f32[1024,3072]{1,0:T(8,128)}), f32[32,3072]{1,0:T(8,128)}) %reduce-scatter.23.cloned.1.call-update) | async-done | bytes 393232 | tf_op jit(solution)/shard_map/reduce_scatter | solution.py:300
  (230 shorter events, 142.5 us)
Async XLA Ops:
  7.2 84.0 %all-gather.9.cloned.1.call-start = ((), (), s32[]{:S(2)}) async-start(), calls=%async_computation.14 | async-start | bytes 6488064 | tf_op jit(solution)/shard_map/all_gather | solution.py:89
  7.9 288.0 %all-gather.11.cloned.1.call-start = ((), (), s32[]{:S(2)}) async-start(), calls=%async_computation.15 | async-start | bytes 2621440 | tf_op jit(solution)/shard_map/all_gather | solution.py:116
  96.0 185.9 %copy-start.27 = (s32[1,128,1]{1,2,0:T(1,128)S(1)}, s32[1,128,1]{1,2,0:T(1,128)}, u32[]{:S(2)}) copy-start(s32[1,128,1]{1,2,0:T(1,128)} %param.25) | copy-start | bytes 1540
  96.0 185.9 %copy-start.37 = (s32[1,1,128]{2,1,0:T(1,128)S(1)}, s32[1,1,128]{2,1,0:T(1,128)}, u32[]{:S(2)}) copy-start(s32[1,1,128]{2,1,0:T(1,128)} %param.26) | copy-start | bytes 1540
  96.0 186.1 %copy-start.41 = (s32[1,7]{1,0:T(1,128)S(1)}, s32[1,7]{1,0:T(1,128)}, u32[]{:S(2)}) copy-start(s32[1,7]{1,0:T(1,128)} %param.28) | copy-start | bytes 88
  96.0 211.6 %all-gather.13.cloned.1.call-start = ((), (), s32[]{:S(2)}) async-start(), calls=%async_computation.16 | async-start | bytes 2162688 | tf_op jit(solution)/shard_map/all_gather | solution.py:90
  96.8 360.5 %all-gather.15.cloned.1.call-start = ((), (), s32[]{:S(2)}) async-start(), calls=%async_computation.17 | async-start | bytes 10485760 | tf_op jit(solution)/shard_map/all_gather | solution.py:98
  97.4 509.2 %all-gather.17.cloned.1.call-start = ((), (), s32[]{:S(2)}) async-start(), calls=%async_computation.18 | async-start | bytes 10485760 | tf_op jit(solution)/shard_map/all_gather | solution.py:208
  98.0 191.3 %collective-permute-start = (bf16[1,1024,1024]{2,1,0:T(8,128)(2,1)S(1)}, bf16[1,1024,1024]{2,1,0:T(8,128)(2,1)}, u32[]{:S(2)}, u32[]{:S(2)}) collective-permute-start(bf16[1,1024,1024]{2,1,0:T(8,128)(2,1)S(1)} %copy-done.3), channel_id=1, source_target_pairs={{0,8},{8,16},{16,24},{24,0},{1,9},{9,17},{17,25},{25,1},{2,10},{10... | collective-permute-start | bytes 6291464 | tf_op jit(solution)/shard_map/ppermute | solution.py:24
  98.0 194.4 %collective-permute-start.1 = (bf16[1,1024,1024]{2,1,0:T(8,128)(2,1)S(1)}, bf16[1,1024,1024]{2,1,0:T(8,128)(2,1)}, u32[]{:S(2)}, u32[]{:S(2)}) collective-permute-start(bf16[1,1024,1024]{2,1,0:T(8,128)(2,1)S(1)} %copy-done.3), channel_id=1, source_target_pairs={{0,24},{8,0},{16,8},{24,16},{1,25},{9,1},{17,9},{25,17},{2,26},{10... | collective-permute-start | bytes 6291464 | tf_op jit(solution)/shard_map/ppermute | solution.py:29
  289.3 95.4 %collective-permute-start.2 = (bf16[1,1024,1024]{2,1,0:T(8,128)(2,1)}, bf16[1,1024,1024]{2,1,0:T(8,128)(2,1)}, u32[]{:S(2)}, u32[]{:S(2)}) collective-permute-start(bf16[1,1024,1024]{2,1,0:T(8,128)(2,1)} %collective-permute-done), channel_id=1, source_target_pairs={{0,8},{8,16},{16,24},{24,0},{1,9},{9,17},{17,25},{25,1},{2,10},{10... | collective-permute-start | bytes 6291464 | tf_op jit(solution)/shard_map/ppermute | solution.py:24
  311.3 76.7 %all-to-all-start = ((bf16[8,18,1024]{2,1,0:T(8,128)(2,1)}), bf16[8,18,1024]{2,1,0:T(8,128)(2,1)S(1)}, u32[]{:S(2)}, u32[]{:S(2)}) async-start(bf16[8,18,1024]{2,1,0:T(8,128)(2,1)} %convolution_convert_fusion.2), calls=%async_computation | async-start | bytes 786432 | tf_op jit(solution)/shard_map/all_to_all | solution.py:186
  463.9 12.0 all-to-all-start.1
  615.3 12.1 all-to-all-start.3
  619.1 61.9 %reduce-scatter.31.cloned.1.call-start = ((), (), s32[]{:S(2)}) async-start(), calls=%async_computation.23 | async-start | bytes 2621440
  640.7 176.1 %reduce-scatter.33.cloned.1.call-start = ((), (), s32[]{:S(2)}) async-start(), calls=%async_computation.24 | async-start | bytes 540672
  643.1 191.6 %reduce-scatter.41.cloned.1.call-start = ((), (), s32[]{:S(2)}) async-start(), calls=%async_computation.28 | async-start | bytes 327680
  645.2 217.3 %reduce-scatter.39.cloned.1.call-start = ((), (), s32[]{:S(2)}) async-start(), calls=%async_computation.27 | async-start | bytes 1310720
  646.8 350.8 %reduce-scatter.35.cloned.1.call-start = ((), (), s32[]{:S(2)}) async-start(), calls=%async_computation.25 | async-start | bytes 540672
  690.4 439.6 %reduce-scatter.37.cloned.1.call-start = ((), (), s32[]{:S(2)}) async-start(), calls=%async_computation.26 | async-start | bytes 540672
  692.6 579.9 %reduce-scatter.29.cloned.1.call-start = ((), (), s32[]{:S(2)}) async-start(), calls=%async_computation.22 | async-start | bytes 10485760 | tf_op jit(solution)/shard_map/reduce_scatter | solution.py:313
  700.0 720.1 %reduce-scatter.27.cloned.1.call-start = ((), (), s32[]{:S(2)}) async-start(), calls=%async_computation.21 | async-start | bytes 10485760 | tf_op jit(solution)/shard_map/reduce_scatter | solution.py:307
  707.0 857.6 %reduce-scatter.25.cloned.1.call-start = ((), (), s32[]{:S(2)}) async-start(), calls=%async_computation.20 | async-start | bytes 4325376 | tf_op jit(solution)/shard_map/reduce_scatter | solution.py:301
  710.7 1011.7 %reduce-scatter.23.cloned.1.call-start = ((), (), s32[]{:S(2)}) async-start(), calls=%async_computation.19 | async-start | bytes 12976128 | tf_op jit(solution)/shard_map/reduce_scatter | solution.py:300
  (39 other events, 883.1 us)
Sparse Core Ops, SparseCore 0:
  10.9 72.2 all-gather.8
  96.1 102.7 all-gather.10
  201.7 60.7 all-gather.12
  263.9 193.2 all-gather.14
  458.7 147.8 all-gather.16
  640.8 40.2 reduce-scatter.30
  683.4 133.3 reduce-scatter.32
  819.1 15.5 reduce-scatter.40
  837.1 25.3 reduce-scatter.38
  865.1 132.4 reduce-scatter.34
  999.9 129.9 reduce-scatter.36
  1132.1 140.3 reduce-scatter.28
  1274.9 145.1 reduce-scatter.26
  1422.8 141.7 reduce-scatter.24
  1571.0 151.2 reduce-scatter.22
